TPU v7x, 32 devices: a whole 2x2x4 slice. The times are simulated.
32 devices in a mesh: cp: 8 (over y, x, core), sp: 4 (over z).
Axes of the slice: x: 2, y: 2, z: 4, core: 2. Of those that a mesh axis runs over, the one named last changes fastest.
Arguments:
- queries: bfloat16 [3072, 2048], P(('cp', 'sp')), may hold values from -6 to 6
- key_vectors: bfloat16 [3072, 512], P(('cp', 'sp')), may hold values from -6 to 6
- value_matrix: bfloat16 [3072, 512], P(('cp', 'sp')), may hold values from -6 to 6
- span_order: int32 [8], replicated, may hold values from 0 to 7, each once
Outputs:
- attended: bfloat16 [3072, 2048], P(('cp', 'sp'))
Inputs may be any that keep to these rules, and one draw needn't show every extreme that they name: `span_order`: each value appears exactly once.
All inputs are finite; a program needn't handle non-finite values.
Results may differ from a plain program's by a relative error of at most 0.0055.
Values may be sent and summed in bfloat16 or wider, within the bound.
A program may use at most 128 MiB of HBM per device.

v0:
```python
import jax
import jax.numpy as jnp
from jax import lax
from jax.sharding import PartitionSpec as P

HEAD_WIDTH = 128
masked_score = -1e30


def span_position(row_ids, span_order, pair_count, span_rows):
    slot_ids = row_ids // span_rows
    pair_ids = slot_ids // 2
    picked = jnp.sum(
        jnp.where(
            pair_ids[:, None] == jnp.arange(pair_count, dtype=jnp.int32)[None, :],
            span_order[None, :],
            0,
        ),
        axis=1,
    )
    span_ids = jnp.where(slot_ids % 2 == 1, 2 * pair_count - 1 - picked, picked)
    return span_ids * span_rows + row_ids % span_rows


def absorb_block(state_in, query_blk, query_pos, key_blk, value_blk, key_pos):
    run_max, run_sum, accumulated = state_in
    scores = jnp.einsum(
        "qhd,kd->hqk", query_blk, key_blk, preferred_element_type=jnp.float32
    ) * query_blk.shape[2] ** (-0.5)
    allowed = key_pos[None, None, :] <= query_pos[None, :, None]
    new_peak = jnp.maximum(run_max, jnp.max(jnp.where(allowed, scores, masked_score), axis=2))
    weights = jnp.where(allowed, jnp.exp(scores - new_peak[:, :, None]), 0.0)
    factor = jnp.exp(run_max - new_peak)
    run_sum = run_sum * factor + jnp.sum(weights, axis=2)
    accumulated = accumulated * factor[:, :, None] + jnp.einsum(
        "hqk,kd->hqd", weights.astype(jnp.bfloat16), value_blk, preferred_element_type=jnp.float32
    )
    return (new_peak, run_sum, accumulated)


def pick_block(key_count, unit_rows):
    block_row_list = unit_rows
    while block_row_list * 2 <= 1024 and key_count % (block_row_list * 2) == 0:
        block_row_list = block_row_list * 2
    return block_row_list


def guarded(state_in, query_blk, query_pos, key_blk, value_blk, key_pos, lowest):

    def compute(states):
        return absorb_block(states, query_blk, query_pos, key_blk, value_blk, key_pos)

    def unchanged(states):
        return states

    return lax.cond(lowest <= jnp.max(query_pos), compute, unchanged, state_in)


def sweep(carries, query_list, key_rows, value_rows, position_of, block_row_list):
    key_count = key_rows.shape[0]

    def advance(states, offset):
        key_blk = lax.dynamic_slice_in_dim(key_rows, offset, block_row_list, 0)
        value_blk = lax.dynamic_slice_in_dim(value_rows, offset, block_row_list, 0)
        key_pos = position_of(offset + jnp.arange(block_row_list, dtype=jnp.int32))
        lowest = jnp.min(key_pos)
        updated = []
        for state_in, entry in zip(states, query_list):
            updated.append(
                guarded(state_in, entry[0], entry[1], key_blk, value_blk, key_pos, lowest)
            )
        return (tuple(updated), None)

    offsets = jnp.arange(key_count // block_row_list, dtype=jnp.int32) * block_row_list
    return lax.scan(advance, carries, offsets)[0]


def per_device(queries, key_vectors, value_matrix, span_order):
    tok_rows = queries.shape[0]
    cp_count = lax.axis_size("cp")
    sp_count = lax.axis_size("sp")
    local_query = lax.all_to_all(queries, "sp", split_axis=1, concat_axis=0, tiled=True)
    group_rows = local_query.shape[0]
    span_rows = group_rows // 2
    head_count = local_query.shape[1] // HEAD_WIDTH
    query_heads = local_query.reshape(group_rows, head_count, HEAD_WIDTH)
    group_id = lax.axis_index("cp")
    query_ids = group_id * group_rows + jnp.arange(group_rows, dtype=jnp.int32)
    query_pos = span_position(query_ids, span_order, cp_count, span_rows)
    query_list = [(query_heads, query_pos)]
    initial = tuple(
        (
            (
                jnp.full((head_count, entry[1].shape[0]), masked_score, jnp.float32),
                jnp.zeros((head_count, entry[1].shape[0]), jnp.float32),
                jnp.zeros((head_count, entry[1].shape[0], HEAD_WIDTH), jnp.float32),
            )
            for entry in query_list
        )
    )
    whole_key, whole_value = (
        lax.all_gather(key_vectors, "cp", axis=0, tiled=True),
        lax.all_gather(value_matrix, "cp", axis=0, tiled=True),
    )
    head_key, head_value = (
        lax.all_to_all(whole_key, "sp", split_axis=1, concat_axis=0, tiled=True),
        lax.all_to_all(whole_value, "sp", split_axis=1, concat_axis=0, tiled=True),
    )
    total_rows = head_key.shape[0]
    span_count = total_rows // span_rows
    slot_ids = jnp.arange(span_count, dtype=jnp.int32)
    pair_pick = jnp.sum(
        jnp.where(
            (slot_ids // 2)[:, None] == jnp.arange(cp_count, dtype=jnp.int32)[None, :],
            span_order[None, :],
            0,
        ),
        axis=1,
    )
    span_of_slot = jnp.where(slot_ids % 2 == 1, 2 * cp_count - 1 - pair_pick, pair_pick)
    slot_of_span = jnp.sum(
        jnp.where(span_of_slot[None, :] == slot_ids[:, None], slot_ids[None, :], 0), axis=1
    )

    def position_layout(rows):
        stored = jnp.transpose(rows.reshape(sp_count, cp_count, tok_rows, HEAD_WIDTH), (1, 0, 2, 3))
        spans = stored.reshape(span_count, span_rows, HEAD_WIDTH)
        return jnp.take(spans, slot_of_span, axis=0).reshape(total_rows, HEAD_WIDTH)

    ordered_key = position_layout(head_key)
    ordered_value = position_layout(head_value)

    def plain_position(row_ids):
        return row_ids

    carries = sweep(
        initial,
        query_list,
        ordered_key,
        ordered_value,
        plain_position,
        pick_block(total_rows, span_rows),
    )
    pieces = [entry[2] / entry[1][:, :, None] for entry in carries]
    joined = pieces[0]
    mixed_rows = (
        jnp.transpose(joined, (1, 0, 2))
        .reshape(group_rows, head_count * HEAD_WIDTH)
        .astype(jnp.bfloat16)
    )
    return lax.all_to_all(mixed_rows, "sp", split_axis=0, concat_axis=1, tiled=True)


def solution(mesh):
    return jax.shard_map(
        per_device,
        mesh=mesh,
        in_specs=(P(("cp", "sp"), None), P(("cp", "sp"), None), P(("cp", "sp"), None), P()),
        out_specs=P(("cp", "sp"), None),
        check_vma=False,
    )
```

profile of v0, /device:TPU:0, one launch (start us, length us, event | category | flops | bytes accessed | tf_op | source)
XLA Modules:
  0.0 125.0 jit_solution(15922890918576906589)
XLA Ops:
  0.0 0.0 copy-start
  0.0 0.0 copy-start.1
  0.0 1.8 %copy.54 = bf16[12,4,8,512]{3,2,0,1:T(8,128)(2,1)} copy(bf16[12,4,8,512]{3,2,1,0:T(8,128)(2,1)} %bitcast.62) | data formatting | bytes 786432 | tf_op jit(solution)/shard_map/all_to_all | solution.py:82
  1.8 6.3 %all-to-all-start.1 = ((bf16[96,4,512]{2,0,1:T(8,128)(2,1)}), bf16[96,4,512]{2,0,1:T(8,128)(2,1)S(1)}, u32[]{:S(2)}, u32[]{:S(2)}) async-start(bf16[96,4,512]{2,0,1:T(8,128)(2,1)} %bitcast.49), calls=%async_computation.1 | async-start | bytes 786432 | tf_op jit(solution)/shard_map/all_to_all | solution.py:82
  8.2 10.7 %all_gather.6 = bf16[768,512]{1,0:T(8,128)(2,1)S(1)} all-gather(bf16[96,512]{1,0:T(8,128)(2,1)} %param.11), channel_id=1, replica_groups=mesh['cp'=8,'sp'=4] {'cp'}, dimensions={0}, use_global_device_ids=true | all-gather | bytes 884736 | tf_op jit(solution)/shard_map/all_gather | solution.py:102
  18.9 1.2 copy.40
  20.1 0.0 all-to-all-done.1
  20.1 5.1 %all-to-all-start = ((bf16[768,4,128]{0,2,1:T(8,128)(2,1)}), bf16[768,4,128]{0,2,1:T(8,128)(2,1)S(1)}, u32[]{:S(2)}, u32[]{:S(2)}) async-start(bf16[768,4,128]{0,2,1:T(8,128)(2,1)} %bitcast.4), calls=%async_computation | async-start | bytes 1572864 | tf_op jit(solution)/shard_map/all_to_all | solution.py:106
  25.2 0.0 copy-done
  25.2 10.0 %all_gather.7 = bf16[768,512]{1,0:T(8,128)(2,1)S(1)} all-gather(bf16[96,512]{1,0:T(8,128)(2,1)S(1)} %copy-done), channel_id=1, replica_groups=mesh['cp'=8,'sp'=4] {'cp'}, dimensions={0}, use_global_device_ids=true | all-gather | bytes 884736 | tf_op jit(solution)/shard_map/all_gather | solution.py:103
  35.2 1.2 copy.44
  36.4 0.0 copy-done.1
  36.4 0.1 select_reduce_fusion.2
  36.5 9.3 %all-to-all-done = bf16[768,4,128]{0,2,1:T(8,128)(2,1)S(1)} async-done(((bf16[768,4,128]{0,2,1:T(8,128)(2,1)}), bf16[768,4,128]{0,2,1:T(8,128)(2,1)S(1)}, u32[]{:S(2)}, u32[]{:S(2)}) %all-to-all-start) | async-done | bytes 786464 | tf_op jit(solution)/shard_map/all_to_all | solution.py:106
  45.8 3.5 %all-to-all-start.2 = ((bf16[768,4,128]{0,2,1:T(8,128)(2,1)}), bf16[768,4,128]{0,2,1:T(8,128)(2,1)S(1)}, u32[]{:S(2)}, u32[]{:S(2)}) async-start(bf16[768,4,128]{0,2,1:T(8,128)(2,1)} %bitcast.11), calls=%async_computation.2 | async-start | bytes 1572864 | tf_op jit(solution)/shard_map/all_to_all | solution.py:107
  49.3 0.1 select_reduce_fusion.1
  49.5 0.1 select_reduce_fusion
  49.5 0.7 fusion.31
  50.3 0.1 reshape.137
  50.4 0.1 copy.47
  50.4 0.4 copy.41
  50.8 0.1 copy.42
  50.9 18.2 %all-to-all-done.2 = bf16[768,4,128]{0,2,1:T(8,128)(2,1)S(1)} async-done(((bf16[768,4,128]{0,2,1:T(8,128)(2,1)}), bf16[768,4,128]{0,2,1:T(8,128)(2,1)S(1)}, u32[]{:S(2)}, u32[]{:S(2)}) %all-to-all-start.2) | async-done | bytes 786464 | tf_op jit(solution)/shard_map/all_to_all | solution.py:107
  69.0 0.4 copy.45
  69.4 0.1 copy.46
  69.5 0.7 gather_fusion
  70.2 0.7 gather_fusion.1
  70.9 1.1 broadcast_select_fusion
  72.0 0.1 broadcast_in_dim.98
  72.1 37.8 %while.15 = (s32[]{:T(128)}, f32[4,384]{1,0:T(4,128)S(1)}, f32[4,384]{1,0:T(4,128)S(1)}, f32[4,384,128]{2,1,0:T(8,128)S(1)}, s32[4]{0:T(128)S(1)}, /*index=5*/s3...) while((s32[]{:T(128)}, f32[4,384]{1,0:T(4,128)S(1)}, ...), condition=%wide.region_10.12_spmd, body=%wide.region_4.11_spmd.sunk | while | flops 617648640 | bytes 17801024 | solution.py:75
  72.1 0.6 dynamic_slice.36
  72.6 1.2 iota_add_fusion.3
  75.1 6.4 %conditional.2 = ((f32[4,384]{1,0:T(4,128)S(1)}, f32[4,384]{1,0:T(4,128)S(1)}, f32[4,384,128]{2,1,0:T(8,128)S(1)})) conditional(s32[]{:T(128)} %convert_element_type.31, (f32[4,384]{1,0:T(4,128)S(1)}, f32[4,384]{1,0:T(4,128)S(1)}, f32[4,384,128]{2,1,0:T(8,128)S(1)}) %tuple.53, (s32[768]{0:T(1024)S(1)}, s32[384]{0:T(512)S(1)}, s32[]{:T(128)}, ...), branch_computations={%region_6.7_spmd, %region_7.10_spmd} | conditional | flops 617647104 | bytes 17797706 | solution.py:56
  76.8 0.2 broadcast_compare_fusion
  77.0 1.0 fusion
  78.0 1.0 fusion.4
  79.0 2.5 %fusion.8 = f32[4,384,128]{2,1,0:T(8,128)S(1)} fusion(f32[768,384,4]{1,0,2:T(8,128)S(1)} %get-tuple-element.282, f32[4,384]{1,0:T(4,128)S(1)} %max.5, pred[384,768]{0,1:T(8,128)(4,1)S(1)} %broadcast_compare_fusion, f32[4,384,128]{2,1,0:T(8,128)S(1)} %get-tuple-element.187, f32[4,384]{1,0:T(4,128)S(1)} %get-tuple-element.278, ...), kind=kOutput, calls=%fused_computation.11 | convolution fusion | flops 307101696 | bytes 6795268 | tf_op jit(solution)/shard_map/while/body/eval_jaxpr/cond/branch_1_fun/hqk,kd->hqd/dot_general | solution.py:35
  81.5 0.6 dynamic_slice.36
  82.1 1.2 iota_add_fusion.3
  84.5 6.4 %conditional.2 = ((f32[4,384]{1,0:T(4,128)S(1)}, f32[4,384]{1,0:T(4,128)S(1)}, f32[4,384,128]{2,1,0:T(8,128)S(1)})) conditional(s32[]{:T(128)} %convert_element_type.31, (f32[4,384]{1,0:T(4,128)S(1)}, f32[4,384]{1,0:T(4,128)S(1)}, f32[4,384,128]{2,1,0:T(8,128)S(1)}) %tuple.53, (s32[768]{0:T(1024)S(1)}, s32[384]{0:T(512)S(1)}, s32[]{:T(128)}, ...), branch_computations={%region_6.7_spmd, %region_7.10_spmd} | conditional | flops 617647104 | bytes 17797706 | solution.py:56
  86.2 0.2 broadcast_compare_fusion
  86.4 1.0 fusion
  87.4 1.0 fusion.4
  88.4 2.5 %fusion.8 = f32[4,384,128]{2,1,0:T(8,128)S(1)} fusion(f32[768,384,4]{1,0,2:T(8,128)S(1)} %get-tuple-element.282, f32[4,384]{1,0:T(4,128)S(1)} %max.5, pred[384,768]{0,1:T(8,128)(4,1)S(1)} %broadcast_compare_fusion, f32[4,384,128]{2,1,0:T(8,128)S(1)} %get-tuple-element.187, f32[4,384]{1,0:T(4,128)S(1)} %get-tuple-element.278, ...), kind=kOutput, calls=%fused_computation.11 | convolution fusion | flops 307101696 | bytes 6795268 | tf_op jit(solution)/shard_map/while/body/eval_jaxpr/cond/branch_1_fun/hqk,kd->hqd/dot_general | solution.py:35
  91.0 0.6 dynamic_slice.36
  91.5 1.2 iota_add_fusion.3
  94.0 6.4 %conditional.2 = ((f32[4,384]{1,0:T(4,128)S(1)}, f32[4,384]{1,0:T(4,128)S(1)}, f32[4,384,128]{2,1,0:T(8,128)S(1)})) conditional(s32[]{:T(128)} %convert_element_type.31, (f32[4,384]{1,0:T(4,128)S(1)}, f32[4,384]{1,0:T(4,128)S(1)}, f32[4,384,128]{2,1,0:T(8,128)S(1)}) %tuple.53, (s32[768]{0:T(1024)S(1)}, s32[384]{0:T(512)S(1)}, s32[]{:T(128)}, ...), branch_computations={%region_6.7_spmd, %region_7.10_spmd} | conditional | flops 617647104 | bytes 17797706 | solution.py:56
  95.6 0.2 broadcast_compare_fusion
  95.9 1.0 fusion
  96.9 1.0 fusion.4
  97.9 2.5 %fusion.8 = f32[4,384,128]{2,1,0:T(8,128)S(1)} fusion(f32[768,384,4]{1,0,2:T(8,128)S(1)} %get-tuple-element.282, f32[4,384]{1,0:T(4,128)S(1)} %max.5, pred[384,768]{0,1:T(8,128)(4,1)S(1)} %broadcast_compare_fusion, f32[4,384,128]{2,1,0:T(8,128)S(1)} %get-tuple-element.187, f32[4,384]{1,0:T(4,128)S(1)} %get-tuple-element.278, ...), kind=kOutput, calls=%fused_computation.11 | convolution fusion | flops 307101696 | bytes 6795268 | tf_op jit(solution)/shard_map/while/body/eval_jaxpr/cond/branch_1_fun/hqk,kd->hqd/dot_general | solution.py:35
  100.4 0.6 dynamic_slice.36
  101.0 1.2 iota_add_fusion.3
  103.4 6.4 %conditional.2 = ((f32[4,384]{1,0:T(4,128)S(1)}, f32[4,384]{1,0:T(4,128)S(1)}, f32[4,384,128]{2,1,0:T(8,128)S(1)})) conditional(s32[]{:T(128)} %convert_element_type.31, (f32[4,384]{1,0:T(4,128)S(1)}, f32[4,384]{1,0:T(4,128)S(1)}, f32[4,384,128]{2,1,0:T(8,128)S(1)}) %tuple.53, (s32[768]{0:T(1024)S(1)}, s32[384]{0:T(512)S(1)}, s32[]{:T(128)}, ...), branch_computations={%region_6.7_spmd, %region_7.10_spmd} | conditional | flops 617647104 | bytes 17797706 | solution.py:56
  105.1 0.2 broadcast_compare_fusion
  105.3 1.0 fusion
  106.3 1.0 fusion.4
  107.3 2.5 %fusion.8 = f32[4,384,128]{2,1,0:T(8,128)S(1)} fusion(f32[768,384,4]{1,0,2:T(8,128)S(1)} %get-tuple-element.282, f32[4,384]{1,0:T(4,128)S(1)} %max.5, pred[384,768]{0,1:T(8,128)(4,1)S(1)} %broadcast_compare_fusion, f32[4,384,128]{2,1,0:T(8,128)S(1)} %get-tuple-element.187, f32[4,384]{1,0:T(4,128)S(1)} %get-tuple-element.278, ...), kind=kOutput, calls=%fused_computation.11 | convolution fusion | flops 307101696 | bytes 6795268 | tf_op jit(solution)/shard_map/while/body/eval_jaxpr/cond/branch_1_fun/hqk,kd->hqd/dot_general | solution.py:35
  109.8 0.3 fusion.21
  110.1 0.3 copy.48
  110.4 0.2 convert_element_type.22
  110.6 13.6 %all_to_all.64 = bf16[4,96,512]{2,1,0:T(8,128)(2,1)S(1)} all-to-all(bf16[4,96,512]{2,1,0:T(8,128)(2,1)S(1)} %convert_element_type.22), channel_id=1, replica_groups=mesh['cp'=8,'sp'=4] {'sp'}, dimensions={0} | all-to-all | bytes 786432 | tf_op jit(solution)/shard_map/all_to_all | solution.py:151
  124.2 0.8 copy.52
  (21 shorter events, 0.2 us)
Async XLA Ops:
  0.0 25.2 %copy-start = (bf16[96,512]{1,0:T(8,128)(2,1)S(1)}, bf16[96,512]{1,0:T(8,128)(2,1)}, u32[]{:S(2)}) copy-start(bf16[96,512]{1,0:T(8,128)(2,1)} %param.12) | copy-start | bytes 294916
  0.0 36.4 %copy-start.1 = (s32[8]{0:T(128)S(1)}, s32[8]{0:T(128)}, u32[]{:S(2)}) copy-start(s32[8]{0:T(128)} %param.13) | copy-start | bytes 100
  1.8 18.3 %all-to-all-start.1 = ((bf16[96,4,512]{2,0,1:T(8,128)(2,1)}), bf16[96,4,512]{2,0,1:T(8,128)(2,1)S(1)}, u32[]{:S(2)}, u32[]{:S(2)}) async-start(bf16[96,4,512]{2,0,1:T(8,128)(2,1)} %bitcast.49), calls=%async_computation.1 | async-start | bytes 786432 | tf_op jit(solution)/shard_map/all_to_all | solution.py:82
  20.1 25.7 %all-to-all-start = ((bf16[768,4,128]{0,2,1:T(8,128)(2,1)}), bf16[768,4,128]{0,2,1:T(8,128)(2,1)S(1)}, u32[]{:S(2)}, u32[]{:S(2)}) async-start(bf16[768,4,128]{0,2,1:T(8,128)(2,1)} %bitcast.4), calls=%async_computation | async-start | bytes 1572864 | tf_op jit(solution)/shard_map/all_to_all | solution.py:106
  45.8 23.2 %all-to-all-start.2 = ((bf16[768,4,128]{0,2,1:T(8,128)(2,1)}), bf16[768,4,128]{0,2,1:T(8,128)(2,1)S(1)}, u32[]{:S(2)}, u32[]{:S(2)}) async-start(bf16[768,4,128]{0,2,1:T(8,128)(2,1)} %bitcast.11), calls=%async_computation.2 | async-start | bytes 1572864 | tf_op jit(solution)/shard_map/all_to_all | solution.py:107
where the time goes:
time: 126 us; the launch traced here: 125 us
  blocking collectives  34.4 us (27%)
  waiting for transfers between devices  27.5 us (22%)
  starting transfers between devices  14.9 us (12%)
  matrix products  13.7 us (11%)
  other arithmetic  12.2 us (10%)
  loops' own time  12 us (10%)
  local copies, waits for them, and re-layouts  10.1 us (8%)
    all_to_all x1, waiting for transfers between devices, per_device(): lax.all_to_all(whole_value, 'sp', split_axis=1, concat_axis=0, tiled=True)  18.2 us
    all_to_all x1, blocking collectives, per_device(): lax.all_to_all(mixed_rows, 'sp', split_axis=0, concat_axis=1, tiled=True)  13.6 us
    all_gather x1, blocking collectives, per_device(): lax.all_gather(key_vectors, 'cp', axis=0, tiled=True)  10.7 us
    all_gather x1, blocking collectives, per_device(): lax.all_gather(value_matrix, 'cp', axis=0, tiled=True)  10 us
    dot_general x4, matrix products, absorb_block(): jnp.einsum('hqk,kd->hqd', weights.astype(jnp.bfloat16), value_blk, prefer...  9.88 us
    all_to_all x1, waiting for transfers between devices, per_device(): lax.all_to_all(whole_key, 'sp', split_axis=1, concat_axis=0, tiled=True)  9.34 us
    another operation x4, loops' own time, guarded(): return lax.cond(lowest <= jnp.max(query_pos), compute, unchanged, state_in)  6.78 us
    all_to_all x1, starting transfers between devices, per_device(): lax.all_to_all(queries, 'sp', split_axis=1, concat_axis=0, tiled=True)  6.35 us
  transfers between devices with their start and end apart: 3, of which 2 were waited for; matrix products, arithmetic and copies ran while one was open for 3% of the time, Pallas kernels for 0%

commit v1 on v0

--- a/solution.py
+++ b/solution.py
@@ -5,6 +5,13 @@
 
 HEAD_WIDTH = 128
 masked_score = -1e30
+
+
+def exchange_blocks(x, name, split, join):
+    size = lax.axis_size(name)
+    pieces = jnp.stack(jnp.split(x, size, axis=split), axis=0)
+    pieces = lax.all_to_all(pieces, name, split_axis=0, concat_axis=0)
+    return jnp.concatenate(pieces, axis=join)
 
 
 def span_position(row_ids, span_order, pair_count, span_rows):
@@ -104,7 +111,7 @@
     )
     head_key, head_value = (
         lax.all_to_all(whole_key, "sp", split_axis=1, concat_axis=0, tiled=True),
-        lax.all_to_all(whole_value, "sp", split_axis=1, concat_axis=0, tiled=True),
+        exchange_blocks(whole_value, "sp", 1, 0),
     )
     total_rows = head_key.shape[0]
     span_count = total_rows // span_rows

time: 126 us -> 123 us (0.976)
  matrix products: 13.7 us -> 10.1 us
  loops' own time: 12 us -> 13.4 us
    dot_general x4, matrix products: 9.88 us -> 6.25 us  [absorb_block(): jnp.einsum('hqk,kd->hqd', weights.astype(jnp.bfloat16), value_blk, prefer...]
    another operation x4, loops' own time: 6.78 us -> 8.48 us  [guarded(): return lax.cond(lowest <= jnp.max(query_pos), compute, unchanged, state_in)]
where the time goes in v1:
time: 123 us; the launch traced here: 122 us
  blocking collectives  34.4 us (28%)
  waiting for transfers between devices  27.5 us (22%)
  starting transfers between devices  14.9 us (12%)
  loops' own time  13.4 us (11%)
  other arithmetic  12.8 us (10%)
  matrix products  10.1 us (8%)
  local copies, waits for them, and re-layouts  9.14 us (7%)
    all_to_all x1, waiting for transfers between devices, exchange_blocks(): pieces = lax.all_to_all(pieces, name, split_axis=0, concat_axis=0)  18.2 us
    all_to_all x1, blocking collectives, per_device(): lax.all_to_all(mixed_rows, 'sp', split_axis=0, concat_axis=1, tiled=True)  13.6 us
    all_gather x1, blocking collectives, per_device(): lax.all_gather(key_vectors, 'cp', axis=0, tiled=True)  10.7 us
    all_gather x1, blocking collectives, per_device(): lax.all_gather(value_matrix, 'cp', axis=0, tiled=True)  10 us
    all_to_all x1, waiting for transfers between devices, per_device(): lax.all_to_all(whole_key, 'sp', split_axis=1, concat_axis=0, tiled=True)  9.37 us
    another operation x4, loops' own time, guarded(): return lax.cond(lowest <= jnp.max(query_pos), compute, unchanged, state_in)  8.48 us
    all_to_all x1, starting transfers between devices, per_device(): lax.all_to_all(queries, 'sp', split_axis=1, concat_axis=0, tiled=True)  6.35 us
    dot_general x4, matrix products, absorb_block(): jnp.einsum('hqk,kd->hqd', weights.astype(jnp.bfloat16), value_blk, prefer...  6.25 us
  transfers between devices with their start and end apart: 3, of which 2 were waited for; matrix products, arithmetic and copies ran while one was open for 3% of the time, Pallas kernels for 0%

profile of v1, /device:TPU:0, one launch (start us, length us, event | category | flops | bytes accessed | tf_op | source)
XLA Modules:
  0.0 122.4 jit_solution(5827007886364631387)
XLA Ops:
  0.0 0.0 copy-start.1
  0.0 0.0 copy-start
  0.0 1.8 %copy.48 = bf16[12,4,8,512]{3,2,0,1:T(8,128)(2,1)} copy(bf16[12,4,8,512]{3,2,1,0:T(8,128)(2,1)} %bitcast.67) | data formatting | bytes 786432 | tf_op jit(solution)/shard_map/all_to_all | solution.py:89
  1.8 6.3 %all-to-all-start.1 = ((bf16[96,4,512]{2,0,1:T(8,128)(2,1)}), bf16[96,4,512]{2,0,1:T(8,128)(2,1)S(1)}, u32[]{:S(2)}, u32[]{:S(2)}) async-start(bf16[96,4,512]{2,0,1:T(8,128)(2,1)} %bitcast.55), calls=%async_computation.1 | async-start | bytes 786432 | tf_op jit(solution)/shard_map/all_to_all | solution.py:89
  8.2 10.7 %all_gather.6 = bf16[768,512]{1,0:T(8,128)(2,1)S(1)} all-gather(bf16[96,512]{1,0:T(8,128)(2,1)} %param.11), channel_id=1, replica_groups=mesh['cp'=8,'sp'=4] {'cp'}, dimensions={0}, use_global_device_ids=true | all-gather | bytes 884736 | tf_op jit(solution)/shard_map/all_gather | solution.py:109
  18.9 1.2 copy.36
  20.1 0.0 all-to-all-done.1
  20.1 5.1 %all-to-all-start = ((bf16[768,4,128]{0,2,1:T(8,128)(2,1)}), bf16[768,4,128]{0,2,1:T(8,128)(2,1)S(1)}, u32[]{:S(2)}, u32[]{:S(2)}) async-start(bf16[768,4,128]{0,2,1:T(8,128)(2,1)} %bitcast.4), calls=%async_computation | async-start | bytes 1572864 | tf_op jit(solution)/shard_map/all_to_all | solution.py:113
  25.2 0.0 copy-done.1
  25.2 0.1 select_reduce_fusion.2
  25.3 0.0 copy-done
  25.3 10.0 %all_gather.7 = bf16[768,512]{1,0:T(8,128)(2,1)S(1)} all-gather(bf16[96,512]{1,0:T(8,128)(2,1)S(1)} %copy-done), channel_id=1, replica_groups=mesh['cp'=8,'sp'=4] {'cp'}, dimensions={0}, use_global_device_ids=true | all-gather | bytes 884736 | tf_op jit(solution)/shard_map/all_gather | solution.py:110
  35.3 0.1 slice_bitcast_fusion.3
  35.5 1.0 pad_maximum_fusion
  36.4 9.4 %all-to-all-done = bf16[768,4,128]{0,2,1:T(8,128)(2,1)S(1)} async-done(((bf16[768,4,128]{0,2,1:T(8,128)(2,1)}), bf16[768,4,128]{0,2,1:T(8,128)(2,1)S(1)}, u32[]{:S(2)}, u32[]{:S(2)}) %all-to-all-start) | async-done | bytes 786464 | tf_op jit(solution)/shard_map/all_to_all | solution.py:113
  45.8 3.5 %all-to-all-start.2 = ((bf16[4,768,128]{2,1,0:T(8,128)(2,1)}), bf16[4,768,128]{2,1,0:T(8,128)(2,1)S(1)}, u32[]{:S(2)}, u32[]{:S(2)}) async-start(bf16[4,768,128]{2,1,0:T(8,128)(2,1)} %pad_maximum_fusion), calls=%async_computation.2 | async-start | bytes 1572864 | tf_op jit(solution)/shard_map/all_to_all | solution.py:13
  49.3 0.1 select_reduce_fusion.1
  49.5 0.1 select_reduce_fusion
  49.5 0.7 fusion.31
  50.3 0.1 reshape.130
  50.4 0.1 copy.41
  50.4 0.4 copy.37
  50.8 0.1 copy.38
  50.9 18.2 %all-to-all-done.2 = bf16[4,768,128]{2,1,0:T(8,128)(2,1)S(1)} async-done(((bf16[4,768,128]{2,1,0:T(8,128)(2,1)}), bf16[4,768,128]{2,1,0:T(8,128)(2,1)S(1)}, u32[]{:S(2)}, u32[]{:S(2)}) %all-to-all-start.2) | async-done | bytes 786464 | tf_op jit(solution)/shard_map/all_to_all | solution.py:13
  69.0 0.1 copy.40
  69.1 0.7 gather_fusion
  69.8 0.7 gather_fusion.1
  70.5 0.2 broadcast_select_fusion
  70.8 0.1 broadcast_in_dim.98
  70.8 36.4 %while.15 = (s32[]{:T(128)}, f32[4,384]{1,0:T(4,128)S(1)}, f32[4,384]{1,0:T(4,128)S(1)}, f32[4,384,128]{2,1,0:T(8,128)S(1)}, s32[4]{0:T(128)S(1)}, /*index=5*/s3...) while((s32[]{:T(128)}, f32[4,384]{1,0:T(4,128)S(1)}, ...), condition=%wide.region_10.12_spmd, body=%wide.region_4.11_spmd.sunk | while | flops 617648640 | bytes 17801024 | solution.py:82
  70.8 0.7 dynamic_slice.36
  71.5 1.3 %iota_add_fusion.3 = (s32[768]{0:T(1024)S(1)}, s32[]{:T(128)}) fusion(s32[]{:T(128)} %bitcast.57), kind=kLoop, calls=%fused_computation.24.clone.2 | loop fusion | flops 1535 | bytes 3080 | tf_op jit(solution)/shard_map/while/body/eval_jaxpr/add | solution.py:72
  74.0 5.9 %conditional.2 = ((f32[4,384]{1,0:T(4,128)S(1)}, f32[4,384]{1,0:T(4,128)S(1)}, f32[4,384,128]{2,1,0:T(8,128)S(1)})) conditional(s32[]{:T(128)} %convert_element_type.31, (f32[4,384]{1,0:T(4,128)S(1)}, f32[4,384]{1,0:T(4,128)S(1)}, f32[4,384,128]{2,1,0:T(8,128)S(1)}) %tuple.56, (s32[768]{0:T(1024)S(1)}, s32[384]{0:T(512)S(1)}, s32[]{:T(128)}, ...), branch_computations={%region_6.7_spmd, %region_7.10_spmd} | conditional | flops 617647104 | bytes 17797706 | solution.py:63
  76.1 0.2 broadcast_compare_fusion
  76.3 1.0 fusion
  77.3 1.0 fusion.4
  78.3 1.6 %fusion.8 = f32[4,384,128]{2,1,0:T(8,128)S(1)} fusion(f32[768,384,4]{1,0,2:T(8,128)S(1)} %get-tuple-element.282, f32[4,384]{1,0:T(4,128)S(1)} %max.5, pred[384,768]{0,1:T(8,128)(4,1)S(1)} %broadcast_compare_fusion, f32[4,384,128]{2,1,0:T(8,128)S(1)} %get-tuple-element.187, f32[4,384]{1,0:T(4,128)S(1)} %get-tuple-element.278, ...), kind=kOutput, calls=%fused_computation.11 | convolution fusion | flops 307101696 | bytes 6795268 | tf_op jit(solution)/shard_map/while/body/eval_jaxpr/cond/branch_1_fun/hqk,kd->hqd/dot_general | solution.py:42
  79.9 0.7 dynamic_slice.36
  80.6 1.3 %iota_add_fusion.3 = (s32[768]{0:T(1024)S(1)}, s32[]{:T(128)}) fusion(s32[]{:T(128)} %bitcast.57), kind=kLoop, calls=%fused_computation.24.clone.2 | loop fusion | flops 1535 | bytes 3080 | tf_op jit(solution)/shard_map/while/body/eval_jaxpr/add | solution.py:72
  83.1 5.9 %conditional.2 = ((f32[4,384]{1,0:T(4,128)S(1)}, f32[4,384]{1,0:T(4,128)S(1)}, f32[4,384,128]{2,1,0:T(8,128)S(1)})) conditional(s32[]{:T(128)} %convert_element_type.31, (f32[4,384]{1,0:T(4,128)S(1)}, f32[4,384]{1,0:T(4,128)S(1)}, f32[4,384,128]{2,1,0:T(8,128)S(1)}) %tuple.56, (s32[768]{0:T(1024)S(1)}, s32[384]{0:T(512)S(1)}, s32[]{:T(128)}, ...), branch_computations={%region_6.7_spmd, %region_7.10_spmd} | conditional | flops 617647104 | bytes 17797706 | solution.py:63
  85.2 0.2 broadcast_compare_fusion
  85.4 1.0 fusion
  86.4 1.0 fusion.4
  87.4 1.6 %fusion.8 = f32[4,384,128]{2,1,0:T(8,128)S(1)} fusion(f32[768,384,4]{1,0,2:T(8,128)S(1)} %get-tuple-element.282, f32[4,384]{1,0:T(4,128)S(1)} %max.5, pred[384,768]{0,1:T(8,128)(4,1)S(1)} %broadcast_compare_fusion, f32[4,384,128]{2,1,0:T(8,128)S(1)} %get-tuple-element.187, f32[4,384]{1,0:T(4,128)S(1)} %get-tuple-element.278, ...), kind=kOutput, calls=%fused_computation.11 | convolution fusion | flops 307101696 | bytes 6795268 | tf_op jit(solution)/shard_map/while/body/eval_jaxpr/cond/branch_1_fun/hqk,kd->hqd/dot_general | solution.py:42
  89.0 0.7 dynamic_slice.36
  89.7 1.3 %iota_add_fusion.3 = (s32[768]{0:T(1024)S(1)}, s32[]{:T(128)}) fusion(s32[]{:T(128)} %bitcast.57), kind=kLoop, calls=%fused_computation.24.clone.2 | loop fusion | flops 1535 | bytes 3080 | tf_op jit(solution)/shard_map/while/body/eval_jaxpr/add | solution.py:72
  92.2 5.9 %conditional.2 = ((f32[4,384]{1,0:T(4,128)S(1)}, f32[4,384]{1,0:T(4,128)S(1)}, f32[4,384,128]{2,1,0:T(8,128)S(1)})) conditional(s32[]{:T(128)} %convert_element_type.31, (f32[4,384]{1,0:T(4,128)S(1)}, f32[4,384]{1,0:T(4,128)S(1)}, f32[4,384,128]{2,1,0:T(8,128)S(1)}) %tuple.56, (s32[768]{0:T(1024)S(1)}, s32[384]{0:T(512)S(1)}, s32[]{:T(128)}, ...), branch_computations={%region_6.7_spmd, %region_7.10_spmd} | conditional | flops 617647104 | bytes 17797706 | solution.py:63
  94.3 0.2 broadcast_compare_fusion
  94.5 1.0 fusion
  95.5 1.0 fusion.4
  96.6 1.6 %fusion.8 = f32[4,384,128]{2,1,0:T(8,128)S(1)} fusion(f32[768,384,4]{1,0,2:T(8,128)S(1)} %get-tuple-element.282, f32[4,384]{1,0:T(4,128)S(1)} %max.5, pred[384,768]{0,1:T(8,128)(4,1)S(1)} %broadcast_compare_fusion, f32[4,384,128]{2,1,0:T(8,128)S(1)} %get-tuple-element.187, f32[4,384]{1,0:T(4,128)S(1)} %get-tuple-element.278, ...), kind=kOutput, calls=%fused_computation.11 | convolution fusion | flops 307101696 | bytes 6795268 | tf_op jit(solution)/shard_map/while/body/eval_jaxpr/cond/branch_1_fun/hqk,kd->hqd/dot_general | solution.py:42
  98.2 0.7 dynamic_slice.36
  98.8 1.3 %iota_add_fusion.3 = (s32[768]{0:T(1024)S(1)}, s32[]{:T(128)}) fusion(s32[]{:T(128)} %bitcast.57), kind=kLoop, calls=%fused_computation.24.clone.2 | loop fusion | flops 1535 | bytes 3080 | tf_op jit(solution)/shard_map/while/body/eval_jaxpr/add | solution.py:72
  101.3 5.9 %conditional.2 = ((f32[4,384]{1,0:T(4,128)S(1)}, f32[4,384]{1,0:T(4,128)S(1)}, f32[4,384,128]{2,1,0:T(8,128)S(1)})) conditional(s32[]{:T(128)} %convert_element_type.31, (f32[4,384]{1,0:T(4,128)S(1)}, f32[4,384]{1,0:T(4,128)S(1)}, f32[4,384,128]{2,1,0:T(8,128)S(1)}) %tuple.56, (s32[768]{0:T(1024)S(1)}, s32[384]{0:T(512)S(1)}, s32[]{:T(128)}, ...), branch_computations={%region_6.7_spmd, %region_7.10_spmd} | conditional | flops 617647104 | bytes 17797706 | solution.py:63
  103.4 0.2 broadcast_compare_fusion
  103.6 1.0 fusion
  104.6 1.0 fusion.4
  105.7 1.6 %fusion.8 = f32[4,384,128]{2,1,0:T(8,128)S(1)} fusion(f32[768,384,4]{1,0,2:T(8,128)S(1)} %get-tuple-element.282, f32[4,384]{1,0:T(4,128)S(1)} %max.5, pred[384,768]{0,1:T(8,128)(4,1)S(1)} %broadcast_compare_fusion, f32[4,384,128]{2,1,0:T(8,128)S(1)} %get-tuple-element.187, f32[4,384]{1,0:T(4,128)S(1)} %get-tuple-element.278, ...), kind=kOutput, calls=%fused_computation.11 | convolution fusion | flops 307101696 | bytes 6795268 | tf_op jit(solution)/shard_map/while/body/eval_jaxpr/cond/branch_1_fun/hqk,kd->hqd/dot_general | solution.py:42
  107.2 0.3 fusion.21
  107.5 0.3 copy.42
  107.8 0.2 convert_element_type.22
  108.0 13.6 %all_to_all.53 = bf16[4,96,512]{2,1,0:T(8,128)(2,1)S(1)} all-to-all(bf16[4,96,512]{2,1,0:T(8,128)(2,1)S(1)} %convert_element_type.22), channel_id=1, replica_groups=mesh['cp'=8,'sp'=4] {'sp'}, dimensions={0} | all-to-all | bytes 786432 | tf_op jit(solution)/shard_map/all_to_all | solution.py:158
  121.6 0.8 copy.46
  (21 shorter events, 0.2 us)
Async XLA Ops:
  0.0 25.2 %copy-start.1 = (s32[8]{0:T(128)S(1)}, s32[8]{0:T(128)}, u32[]{:S(2)}) copy-start(s32[8]{0:T(128)} %param.13) | copy-start | bytes 100
  0.0 25.3 %copy-start = (bf16[96,512]{1,0:T(8,128)(2,1)S(1)}, bf16[96,512]{1,0:T(8,128)(2,1)}, u32[]{:S(2)}) copy-start(bf16[96,512]{1,0:T(8,128)(2,1)} %param.12) | copy-start | bytes 294916
  1.8 18.3 %all-to-all-start.1 = ((bf16[96,4,512]{2,0,1:T(8,128)(2,1)}), bf16[96,4,512]{2,0,1:T(8,128)(2,1)S(1)}, u32[]{:S(2)}, u32[]{:S(2)}) async-start(bf16[96,4,512]{2,0,1:T(8,128)(2,1)} %bitcast.55), calls=%async_computation.1 | async-start | bytes 786432 | tf_op jit(solution)/shard_map/all_to_all | solution.py:89
  20.1 25.7 %all-to-all-start = ((bf16[768,4,128]{0,2,1:T(8,128)(2,1)}), bf16[768,4,128]{0,2,1:T(8,128)(2,1)S(1)}, u32[]{:S(2)}, u32[]{:S(2)}) async-start(bf16[768,4,128]{0,2,1:T(8,128)(2,1)} %bitcast.4), calls=%async_computation | async-start | bytes 1572864 | tf_op jit(solution)/shard_map/all_to_all | solution.py:113
  45.8 23.2 %all-to-all-start.2 = ((bf16[4,768,128]{2,1,0:T(8,128)(2,1)}), bf16[4,768,128]{2,1,0:T(8,128)(2,1)S(1)}, u32[]{:S(2)}, u32[]{:S(2)}) async-start(bf16[4,768,128]{2,1,0:T(8,128)(2,1)} %pad_maximum_fusion), calls=%async_computation.2 | async-start | bytes 1572864 | tf_op jit(solution)/shard_map/all_to_all | solution.py:13
